TPU v7x, 32 devices: a whole 2x2x4 slice. The times are simulated.
32 devices in a mesh: view: 4 (over y, core), row: 8 (over z, x).
Axes of the slice: x: 2, y: 2, z: 4, core: 2. Of those that a mesh axis runs over, the one named last changes fastest.
Arguments:
- features: float32 [4, 16384, 2048], P('view', 'row'), may hold values from -0.125 to 0.125
- view_maps: float32 [4, 2048, 256], P('view', 'row'), may hold values from -6 to 6
- shared: float32 [16384, 256], P('row'), may hold values from -6 to 6
Outputs:
- maps_out: float32 [4, 2048, 256], P('view', 'row')
- shared_out: float32 [16384, 256], P('row')
All inputs are finite; a program needn't handle non-finite values.
Results may differ from a plain program's by a relative error of at most 0.00013.
Values sent between devices are 32-bit elements; how exact they have to be, the bound alone decides.
A program may use at most 128 MiB of HBM per device.

v0:
```python
import jax
import jax.numpy as jnp
from jax import lax
from jax.sharding import PartitionSpec as P

ITERS = 2
NEWTON = 5
step_rate = 0.5


def newton_root(gram_matrix):
    highest = lax.Precision.HIGHEST
    frob_norm = jnp.sqrt(jnp.sum(gram_matrix * gram_matrix))
    scaled = gram_matrix / frob_norm
    identity = jnp.eye(gram_matrix.shape[0], dtype=jnp.float32)
    inverse_root = identity
    for newton_step in range(NEWTON):
        correction = 1.5 * identity - 0.5 * jnp.dot(inverse_root, scaled, precision=highest)
        scaled = jnp.dot(scaled, correction, precision=highest)
        inverse_root = jnp.dot(correction, inverse_root, precision=highest)
    return (inverse_root, frob_norm)


def local(features, view_maps, shared):
    highest = lax.Precision.HIGHEST
    samples = features[0]
    map_shard = view_maps[0]
    local_rows = samples.shape[0]
    width = samples.shape[1]
    shard_rows = map_shard.shape[0]
    total_rows = local_rows * lax.axis_size("row")
    view_count = lax.axis_size("view")
    step_size = step_rate * width / total_rows
    whole_map = lax.all_gather(map_shard, "row", axis=0, tiled=True)
    projected = jnp.dot(samples, whole_map, precision=highest)
    for iteration in range(ITERS):
        residual = projected - shared
        gradient = lax.psum(jnp.dot(samples.T, residual, precision=highest), "row")
        whole_map = whole_map - step_size * gradient
        projected = jnp.dot(samples, whole_map, precision=highest)
        average = lax.psum(projected, "view") / view_count
        gram_matrix = lax.psum(jnp.dot(average.T, average, precision=highest), "row")
        inverse_root, frob_norm = newton_root(gram_matrix)
        shared = jnp.dot(average, inverse_root, precision=highest) * jnp.sqrt(
            total_rows / frob_norm
        )
    map_shard = lax.dynamic_slice_in_dim(
        whole_map, lax.axis_index("row") * shard_rows, shard_rows, 0
    )
    return (map_shard[None], shared)


def solution(mesh):
    in_specs = (P("view", "row", None), P("view", "row", None), P("row", None))
    out_specs = (P("view", "row", None), P("row", None))
    return jax.shard_map(local, mesh=mesh, in_specs=in_specs, out_specs=out_specs, check_vma=False)
```

profile of v0, /device:TPU:0, one launch (start us, length us, event | category | flops | bytes accessed | tf_op | source)
XLA Modules:
  0.0 663.0 jit_solution(7803501747945105830)
XLA Ops:
  7.2 0.0 all-gather.3.cloned.1.call-start
  7.2 1.8 copy.6
  9.0 0.0 all-gather.3.cloned.1.call-update
  9.0 0.0 all-reduce.7.cloned.1.call-start
  9.1 54.6 %all-gather.3.cloned.1.call-done = f32[1,2048,256]{1,2,0:T(8,128)} async-done(((f32[1,256,256]{1,2,0:T(8,128)}), f32[1,2048,256]{1,2,0:T(8,128)}) %all-gather.3.cloned.1.call-update) | async-done | bytes 2097168 | tf_op jit(solution)/shard_map/all_gather | solution.py:34
  63.7 17.4 %fusion.23 = f32[2048,256]{1,0:T(8,128)S(1)} fusion(f32[2048,256]{1,0:T(8,128)} %param.5, f32[1,2048,2048]{2,1,0:T(8,128)} %param.3, f32[1,2048,256]{1,2,0:T(8,128)} %all-gather.3.cloned.1.call-done), kind=kOutput, calls=%fused_computation.17 | convolution fusion | flops 12885426176 | bytes 23068672 | tf_op jit(solution)/shard_map/dot_general | solution.py:35
  81.1 31.3 %fusion.10 = f32[2048,256]{0,1:T(8,128)} fusion(f32[2048,256]{1,0:T(8,128)S(1)} %fusion.23, f32[1,2048,2048]{2,1,0:T(8,128)S(1)} %copy-done), kind=kOutput, calls=%fused_computation.10 | convolution fusion | flops 12884901888 | bytes 20971520 | tf_op jit(solution)/shard_map/dot_general | solution.py:38
  112.4 0.0 all-reduce.7.cloned.1.call-update
  112.4 0.0 all-reduce.9.cloned.1.call-start
  112.5 100.6 %all-reduce.7.cloned.1.call-done = f32[2048,256]{0,1:T(8,128)} async-done(((f32[2048,256]{0,1:T(8,128)}), f32[2048,256]{0,1:T(8,128)}) %all-reduce.7.cloned.1.call-update) | async-done | bytes 2097168 | tf_op jit(solution)/shard_map/psum | solution.py:38
  213.1 18.8 %fusion.13 = f32[2048,256]{0,1:T(8,128)} fusion(f32[1,2048,2048]{2,1,0:T(8,128)} %param.3, f32[1,2048,256]{1,2,0:T(8,128)S(1)} %copy-done.1, f32[2048,256]{0,1:T(8,128)} %all-reduce.7.cloned.1.call-done), kind=kOutput, calls=%fused_computation.11 | convolution fusion | flops 12885950464 | bytes 23068672 | tf_op jit(solution)/shard_map/dot_general | solution.py:40
  231.9 0.0 all-reduce.9.cloned.1.call-update
  231.9 0.0 all-reduce.11.cloned.1.call-start
  232.0 50.8 %all-reduce.9.cloned.1.call-done = f32[2048,256]{0,1:T(8,128)} async-done(((f32[2048,256]{0,1:T(8,128)}), f32[2048,256]{0,1:T(8,128)}) %all-reduce.9.cloned.1.call-update) | async-done | bytes 2097168 | tf_op jit(solution)/shard_map/psum | solution.py:41
  282.8 4.9 fusion.31
  287.6 0.0 all-reduce.11.cloned.1.call-update
  287.7 0.0 all-reduce.13.cloned.1.call-start
  287.7 71.2 %all-reduce.11.cloned.1.call-done = f32[256,256]{1,0:T(8,128)} async-done(((f32[256,256]{1,0:T(8,128)}), f32[256,256]{1,0:T(8,128)}) %all-reduce.11.cloned.1.call-update) | async-done | bytes 262160 | tf_op jit(solution)/shard_map/psum | solution.py:42
  358.9 1.6 multiply_reduce_fusion.1
  361.3 1.3 fusion.42
  362.5 0.3 fusion.48
  362.8 1.3 fusion.49
  364.2 0.4 fusion.41
  364.5 0.4 fusion.57
  364.9 0.4 fusion.56
  365.3 0.4 fusion.40
  365.7 0.4 fusion.59
  366.1 0.4 fusion.58
  366.5 0.4 fusion.39
  366.9 0.4 fusion.61
  367.3 0.4 fusion.60
  367.6 0.4 fusion.38
  368.0 0.4 fusion.62
  368.5 4.4 fusion.22
  372.9 17.8 %fusion.16 = f32[2048,256]{0,1:T(8,128)} fusion(f32[2048,256]{0,1:T(8,128)S(1)} %fusion.22, f32[1,2048,2048]{2,1,0:T(8,128)} %param.3), kind=kOutput, calls=%fused_computation.12 | convolution fusion | flops 12884901888 | bytes 20971520 | tf_op jit(solution)/shard_map/dot_general | solution.py:38
  390.7 0.0 all-reduce.15.cloned.1.call-start
  390.7 101.6 %all-reduce.13.cloned.1.call-done = f32[2048,256]{0,1:T(8,128)} async-done(((f32[2048,256]{0,1:T(8,128)}), f32[2048,256]{0,1:T(8,128)}) %all-reduce.13.cloned.1.call-update) | async-done | bytes 2097168 | tf_op jit(solution)/shard_map/psum | solution.py:38
  492.4 2.8 multiply_subtract_fusion
  495.2 1.3 copy-done.2
  496.5 17.9 %fusion.19 = f32[2048,256]{0,1:T(8,128)} fusion(f32[2048,256]{0,1:T(8,128)S(1)} %multiply_subtract_fusion, f32[1,2048,2048]{2,1,0:T(8,128)} %param.3), kind=kOutput, calls=%fused_computation.13 | convolution fusion | flops 12884901888 | bytes 20971520 | tf_op jit(solution)/shard_map/dot_general | solution.py:40
  514.4 0.0 all-reduce.15.cloned.1.call-update
  514.4 0.3 all-reduce.17.cloned.1.call-start
  514.7 50.6 %all-reduce.15.cloned.1.call-done = f32[2048,256]{0,1:T(8,128)} async-done(((f32[2048,256]{0,1:T(8,128)}), f32[2048,256]{0,1:T(8,128)}) %all-reduce.15.cloned.1.call-update) | async-done | bytes 2097168 | tf_op jit(solution)/shard_map/psum | solution.py:41
  565.2 4.9 fusion.28
  570.1 0.0 all-reduce.17.cloned.1.call-update
  570.1 1.0 constant_dynamic-slice_fusion
  571.1 0.8 copy.7
  572.0 69.4 %all-reduce.17.cloned.1.call-done = f32[256,256]{1,0:T(8,128)} async-done(((f32[256,256]{1,0:T(8,128)}), f32[256,256]{1,0:T(8,128)}) %all-reduce.17.cloned.1.call-update) | async-done | bytes 262160 | tf_op jit(solution)/shard_map/psum | solution.py:42
  641.4 1.6 multiply_reduce_fusion
  643.7 1.3 fusion.37
  645.0 0.3 fusion.47
  645.3 1.3 fusion.50
  646.6 0.4 fusion.36
  647.0 0.4 fusion.64
  647.4 0.4 fusion.63
  647.8 0.4 fusion.35
  648.2 0.4 fusion.66
  648.6 0.4 fusion.65
  649.0 0.4 fusion.34
  649.3 0.4 fusion.68
  649.7 0.4 fusion.67
  650.2 0.4 fusion.33
  650.5 0.4 fusion.69
  651.0 4.8 convolution_multiply_fusion
  (8 shorter events, 0.0 us)
Async XLA Ops:
  7.2 56.5 %all-gather.3.cloned.1.call-start = ((), (), s32[]{:S(2)}) async-start(), calls=%async_computation.6 | async-start | bytes 2359296 | tf_op jit(solution)/shard_map/all_gather | solution.py:34
  9.0 204.1 %all-reduce.7.cloned.1.call-start = ((), (), s32[]{:S(2)}) async-start(), calls=%async_computation | async-start | bytes 4194304 | tf_op jit(solution)/shard_map/psum | solution.py:38
  63.7 17.4 %copy-start = (f32[1,2048,2048]{2,1,0:T(8,128)S(1)}, f32[1,2048,2048]{2,1,0:T(8,128)}, u32[]{:S(2)}) copy-start(f32[1,2048,2048]{2,1,0:T(8,128)} %param.3) | copy-start | bytes 50331652
  112.4 100.7 %copy-start.1 = (f32[1,2048,256]{1,2,0:T(8,128)S(1)}, f32[1,2048,256]{1,2,0:T(8,128)}, u32[]{:S(2)}) copy-start(f32[1,2048,256]{1,2,0:T(8,128)} %all-gather.3.cloned.1.call-done) | copy-start | bytes 6291460
  112.4 170.4 %all-reduce.9.cloned.1.call-start = ((), (), s32[]{:S(2)}) async-start(), calls=%async_computation.1 | async-start | bytes 4194304 | tf_op jit(solution)/shard_map/psum | solution.py:41
  231.9 127.0 %all-reduce.11.cloned.1.call-start = ((), (), s32[]{:S(2)}) async-start(), calls=%async_computation.2 | async-start | bytes 524288 | tf_op jit(solution)/shard_map/psum | solution.py:42
  287.7 204.7 %all-reduce.13.cloned.1.call-start = ((), (), s32[]{:S(2)}) async-start(), calls=%async_computation.3 | async-start | bytes 4194304 | tf_op jit(solution)/shard_map/psum | solution.py:38
  390.7 174.6 %all-reduce.15.cloned.1.call-start = ((), (), s32[]{:S(2)}) async-start(), calls=%async_computation.4 | async-start | bytes 4194304 | tf_op jit(solution)/shard_map/psum | solution.py:41
  495.2 1.3 copy-start.2
  514.4 127.0 %all-reduce.17.cloned.1.call-start = ((), (), s32[]{:S(2)}) async-start(), calls=%async_computation.5 | async-start | bytes 524288 | tf_op jit(solution)/shard_map/psum | solution.py:42
  648.9 2.0 copy-start.3
Sparse Core Ops, SparseCore 0:
  10.6 53.0 all-gather.2
  112.5 100.5 all-reduce.6
  232.1 50.6 all-reduce.8
  287.8 71.0 all-reduce.10
  390.8 101.5 all-reduce.12
  514.5 50.6 all-reduce.14
  570.3 71.0 all-reduce.16
where the time goes:
time: 667 us; the launch traced here: 663 us
  waiting for transfers between devices  499 us (75%)
  matrix products  136 us (20%)
  between operations  16.4 us (2%)
    psum x2, waiting for transfers between devices, local(): gradient = lax.psum(jnp.dot(samples.T, residual, precision=highest), 'row')  202 us
    psum x2, waiting for transfers between devices, local(): lax.psum(jnp.dot(average.T, average, precision=highest), 'row')  141 us
    psum x2, waiting for transfers between devices, local(): average = lax.psum(projected, 'view') / view_count  101 us
    all_gather x1, waiting for transfers between devices, local(): whole_map = lax.all_gather(map_shard, 'row', axis=0, tiled=True)  54.6 us
    dot_general x3, matrix products, local(): projected = jnp.dot(samples, whole_map, precision=highest)  54.1 us
    dot_general x2, matrix products, local(): gradient = lax.psum(jnp.dot(samples.T, residual, precision=highest), 'row')  49.1 us
  transfers between devices with their start and end apart: 7, of which 7 were waited for; matrix products, arithmetic and copies ran while one was open for 0% of the time, Pallas kernels for 0%

commit v1 on v0

--- a/solution.py
+++ b/solution.py
@@ -31,7 +31,8 @@
     total_rows = local_rows * lax.axis_size("row")
     view_count = lax.axis_size("view")
     step_size = step_rate * width / total_rows
-    whole_map = lax.all_gather(map_shard, "row", axis=0, tiled=True)
+    copies = jnp.concatenate([map_shard] * lax.axis_size("row"), axis=0)
+    whole_map = lax.all_to_all(copies, "row", 0, 0, tiled=True)
     projected = jnp.dot(samples, whole_map, precision=highest)
     for iteration in range(ITERS):
         residual = projected - shared

time: 667 us -> 663 us (level)
  matrix products: 136 us -> 120 us
  local copies, waits for them, and re-layouts: 4.92 us -> 15.3 us
  waiting for transfers between devices: 499 us -> 490 us
  starting transfers between devices: 0.5 us -> 8.38 us
    all_gather x1 -> x0, waiting for transfers between devices: 54.6 us -> none  [local(): whole_map = lax.all_gather(map_shard, 'row', axis=0, tiled=True)]
    all_to_all x0 -> x1, waiting for transfers between devices: none -> 45.3 us  [local(): whole_map = lax.all_to_all(copies, 'row', 0, 0, tiled=True)]
    dot_general x2, matrix products: 49.1 us -> 33.4 us  [local(): gradient = lax.psum(jnp.dot(samples.T, residual, precision=highest), 'row')]
    all_to_all x0 -> x1, starting transfers between devices: none -> 7.28 us  [local(): whole_map = lax.all_to_all(copies, 'row', 0, 0, tiled=True)]
  transfers between devices with their start and end apart: 7 -> 7, of which waited for: 7 -> 7; matrix products, arithmetic and copies ran while one was open for 0% -> 1% of each run, Pallas kernels for 0% -> 0%
where the time goes in v1:
time: 663 us; the launch traced here: 656 us
  waiting for transfers between devices  490 us (74%)
  matrix products  120 us (18%)
  between operations  16.3 us (2%)
  local copies, waits for them, and re-layouts  15.3 us (2%)
  starting transfers between devices  8.38 us (1%)
    psum x2, waiting for transfers between devices, local(): gradient = lax.psum(jnp.dot(samples.T, residual, precision=highest), 'row')  202 us
    psum x2, waiting for transfers between devices, local(): lax.psum(jnp.dot(average.T, average, precision=highest), 'row')  140 us
    psum x2, waiting for transfers between devices, local(): average = lax.psum(projected, 'view') / view_count  102 us
    dot_general x3, matrix products, local(): projected = jnp.dot(samples, whole_map, precision=highest)  54 us
    all_to_all x1, waiting for transfers between devices, local(): whole_map = lax.all_to_all(copies, 'row', 0, 0, tiled=True)  45.3 us
    dot_general x2, matrix products, local(): gradient = lax.psum(jnp.dot(samples.T, residual, precision=highest), 'row')  33.4 us
  transfers between devices with their start and end apart: 7, of which 7 were waited for; matrix products, arithmetic and copies ran while one was open for 1% of the time, Pallas kernels for 0%

profile of v1, /device:TPU:0, one launch (start us, length us, event | category | flops | bytes accessed | tf_op | source)
XLA Modules:
  0.0 656.2 jit_solution(5307656627167751612)
XLA Ops:
  7.2 1.0 bitcast_dynamic-update-slice_fusion.6
  8.2 1.0 bitcast_dynamic-update-slice_fusion.5
  9.2 1.0 bitcast_dynamic-update-slice_fusion.4
  10.2 1.0 bitcast_dynamic-update-slice_fusion.3
  11.3 1.8 copy.12
  13.1 7.3 %all-to-all-start = ((f32[8,256,256]{1,2,0:T(8,128)}), f32[8,256,256]{1,2,0:T(8,128)S(1)}, u32[]{:S(2)}, u32[]{:S(2)}) async-start(f32[8,256,256]{1,2,0:T(8,128)} %copy.12), calls=%async_computation | async-start | bytes 4194304 | tf_op jit(solution)/shard_map/all_to_all | solution.py:35
  20.4 2.9 copy.14
  23.3 45.3 %all-to-all-done = f32[8,256,256]{1,2,0:T(8,128)S(1)} async-done(((f32[8,256,256]{1,2,0:T(8,128)}), f32[8,256,256]{1,2,0:T(8,128)S(1)}, u32[]{:S(2)}, u32[]{:S(2)}) %all-to-all-start) | async-done | bytes 2097184 | tf_op jit(solution)/shard_map/all_to_all | solution.py:35
  68.6 1.3 copy-done.3
  69.9 2.0 copy.18
  72.0 17.3 %fusion.26 = f32[2048,256]{0,1:T(8,128)S(1)} fusion(f32[2048,256]{0,1:T(8,128)} %copy.14, f32[2048,256]{0,1:T(8,128)S(1)} %bitcast.104, f32[1,2048,2048]{2,1,0:T(8,128)} %param.3), kind=kOutput, calls=%fused_computation.18 | convolution fusion | flops 12885426176 | bytes 23068672 | tf_op jit(solution)/shard_map/dot_general | solution.py:36
  89.3 15.6 %fusion.13 = f32[2048,256]{0,1:T(8,128)} fusion(f32[2048,256]{0,1:T(8,128)S(1)} %fusion.26, f32[1,2048,2048]{2,1,0:T(8,128)S(1)} %bitcast.103), kind=kOutput, calls=%fused_computation.11 | convolution fusion | flops 12884901888 | bytes 20971520 | tf_op jit(solution)/shard_map/dot_general | solution.py:39
  104.9 0.5 all-reduce.9.cloned.1.call-start
  105.4 101.0 %all-reduce.7.cloned.1.call-done = f32[2048,256]{0,1:T(8,128)} async-done(((f32[2048,256]{0,1:T(8,128)}), f32[2048,256]{0,1:T(8,128)}) %all-reduce.7.cloned.1.call-update) | async-done | bytes 2097168 | tf_op jit(solution)/shard_map/psum | solution.py:39
  206.5 18.8 %fusion.16 = f32[2048,256]{0,1:T(8,128)} fusion(f32[1,2048,2048]{2,1,0:T(8,128)} %param.3, f32[2048,256]{0,1:T(8,128)S(1)} %bitcast.105, f32[2048,256]{0,1:T(8,128)} %all-reduce.7.cloned.1.call-done), kind=kOutput, calls=%fused_computation.12 | convolution fusion | flops 12885950464 | bytes 23068672 | tf_op jit(solution)/shard_map/dot_general | solution.py:41
  225.3 0.0 all-reduce.11.cloned.1.call-start
  225.4 50.8 %all-reduce.9.cloned.1.call-done = f32[2048,256]{0,1:T(8,128)} async-done(((f32[2048,256]{0,1:T(8,128)}), f32[2048,256]{0,1:T(8,128)}) %all-reduce.9.cloned.1.call-update) | async-done | bytes 2097168 | tf_op jit(solution)/shard_map/psum | solution.py:42
  276.2 4.9 fusion.33
  281.1 0.2 all-reduce.13.cloned.1.call-start
  281.3 71.0 %all-reduce.11.cloned.1.call-done = f32[256,256]{1,0:T(8,128)} async-done(((f32[256,256]{1,0:T(8,128)}), f32[256,256]{1,0:T(8,128)}) %all-reduce.11.cloned.1.call-update) | async-done | bytes 262160 | tf_op jit(solution)/shard_map/psum | solution.py:43
  352.3 1.6 multiply_reduce_fusion.1
  354.6 1.3 fusion.44
  355.9 0.3 fusion.50
  356.2 1.3 fusion.51
  357.5 0.4 fusion.43
  357.9 0.4 fusion.59
  358.3 0.4 fusion.58
  358.7 0.4 fusion.42
  359.1 0.4 fusion.61
  359.5 0.4 fusion.60
  359.9 0.4 fusion.41
  360.3 0.4 fusion.63
  360.6 0.4 fusion.62
  361.0 0.4 fusion.40
  361.4 0.4 fusion.64
  361.9 4.3 fusion.25
  366.3 17.8 %fusion.19 = f32[2048,256]{0,1:T(8,128)} fusion(f32[2048,256]{0,1:T(8,128)S(1)} %fusion.25, f32[1,2048,2048]{2,1,0:T(8,128)} %param.3), kind=kOutput, calls=%fused_computation.13 | convolution fusion | flops 12884901888 | bytes 20971520 | tf_op jit(solution)/shard_map/dot_general | solution.py:39
  384.1 0.3 all-reduce.15.cloned.1.call-start
  384.3 101.4 %all-reduce.13.cloned.1.call-done = f32[2048,256]{0,1:T(8,128)} async-done(((f32[2048,256]{0,1:T(8,128)}), f32[2048,256]{0,1:T(8,128)}) %all-reduce.13.cloned.1.call-update) | async-done | bytes 2097168 | tf_op jit(solution)/shard_map/psum | solution.py:39
  485.7 2.8 multiply_subtract_fusion
  488.6 1.3 copy-done.1
  489.9 17.8 %fusion.22 = f32[2048,256]{0,1:T(8,128)} fusion(f32[2048,256]{0,1:T(8,128)S(1)} %multiply_subtract_fusion, f32[1,2048,2048]{2,1,0:T(8,128)} %param.3), kind=kOutput, calls=%fused_computation.14 | convolution fusion | flops 12884901888 | bytes 20971520 | tf_op jit(solution)/shard_map/dot_general | solution.py:41
  507.8 0.0 all-reduce.17.cloned.1.call-start
  507.8 50.8 %all-reduce.15.cloned.1.call-done = f32[2048,256]{0,1:T(8,128)} async-done(((f32[2048,256]{0,1:T(8,128)}), f32[2048,256]{0,1:T(8,128)}) %all-reduce.15.cloned.1.call-update) | async-done | bytes 2097168 | tf_op jit(solution)/shard_map/psum | solution.py:42
  558.6 4.9 fusion.30
  563.5 1.0 constant_dynamic-slice_fusion
  564.5 0.8 copy.16
  565.3 69.4 %all-reduce.17.cloned.1.call-done = f32[256,256]{1,0:T(8,128)} async-done(((f32[256,256]{1,0:T(8,128)}), f32[256,256]{1,0:T(8,128)}) %all-reduce.17.cloned.1.call-update) | async-done | bytes 262160 | tf_op jit(solution)/shard_map/psum | solution.py:43
  634.8 1.6 multiply_reduce_fusion
  637.1 1.3 fusion.39
  638.3 0.3 fusion.49
  638.6 1.3 fusion.52
  640.0 0.4 fusion.38
  640.4 0.4 fusion.66
  640.7 0.4 fusion.65
  641.1 0.4 fusion.37
  641.5 0.4 fusion.68
  641.9 0.4 fusion.67
  642.3 0.4 fusion.36
  642.7 0.4 fusion.70
  643.1 0.4 fusion.69
  643.5 0.4 fusion.35
  643.9 0.4 fusion.71
  644.3 4.8 convolution_multiply_fusion
  (26 shorter events, 0.2 us)
Async XLA Ops:
  7.2 4.0 copy-start
  13.1 55.5 %all-to-all-start = ((f32[8,256,256]{1,2,0:T(8,128)}), f32[8,256,256]{1,2,0:T(8,128)S(1)}, u32[]{:S(2)}, u32[]{:S(2)}) async-start(f32[8,256,256]{1,2,0:T(8,128)} %copy.12), calls=%async_computation | async-start | bytes 4194304 | tf_op jit(solution)/shard_map/all_to_all | solution.py:35
  20.3 186.1 %all-reduce.7.cloned.1.call-start = ((), (), s32[]{:S(2)}) async-start(), calls=%async_computation.1 | async-start | bytes 4194304 | tf_op jit(solution)/shard_map/psum | solution.py:39
  68.6 1.3 copy-start.3
  69.9 19.4 %slice-start = ((s8[16777216]{0:T(1024)(128)(4,1)}), s8[4194304]{0:T(1024)(128)(4,1)S(1)}, s32[]{:S(2)}) async-start(s8[16777216]{0:T(1024)(128)(4,1)} %bitcast.102), calls=%async_computation.7 | async-start | bytes 8388608
  71.9 17.4 %slice-start.1 = ((s8[16777216]{0:T(1024)(128)(4,1)}), s8[4194304]{0:T(1024)(128)(4,1)S(1)}, s32[]{:S(2)}) async-start(s8[16777216]{0:T(1024)(128)(4,1)} %bitcast.102), calls=%async_computation.8 | async-start | bytes 8388608
  71.9 17.3 %slice-start.2 = ((s8[16777216]{0:T(1024)(128)(4,1)}), s8[4194304]{0:T(1024)(128)(4,1)S(1)}, s32[]{:S(2)}) async-start(s8[16777216]{0:T(1024)(128)(4,1)} %bitcast.102), calls=%async_computation.9 | async-start | bytes 8388608
  71.9 17.3 %slice-start.3 = ((s8[16777216]{0:T(1024)(128)(4,1)}), s8[4194304]{0:T(1024)(128)(4,1)S(1)}, s32[]{:S(2)}) async-start(s8[16777216]{0:T(1024)(128)(4,1)} %bitcast.102), calls=%async_computation.10 | async-start | bytes 8388608
  104.9 171.2 %all-reduce.9.cloned.1.call-start = ((), (), s32[]{:S(2)}) async-start(), calls=%async_computation.2 | async-start | bytes 4194304 | tf_op jit(solution)/shard_map/psum | solution.py:42
  225.3 127.0 %all-reduce.11.cloned.1.call-start = ((), (), s32[]{:S(2)}) async-start(), calls=%async_computation.3 | async-start | bytes 524288 | tf_op jit(solution)/shard_map/psum | solution.py:43
  281.1 204.7 %all-reduce.13.cloned.1.call-start = ((), (), s32[]{:S(2)}) async-start(), calls=%async_computation.4 | async-start | bytes 4194304 | tf_op jit(solution)/shard_map/psum | solution.py:39
  384.1 174.5 %all-reduce.15.cloned.1.call-start = ((), (), s32[]{:S(2)}) async-start(), calls=%async_computation.5 | async-start | bytes 4194304 | tf_op jit(solution)/shard_map/psum | solution.py:42
  488.6 1.3 copy-start.1
  507.8 127.0 %all-reduce.17.cloned.1.call-start = ((), (), s32[]{:S(2)}) async-start(), calls=%async_computation.6 | async-start | bytes 524288 | tf_op jit(solution)/shard_map/psum | solution.py:43
  642.3 2.0 copy-start.2
Sparse Core Ops, SparseCore 0:
  105.0 101.3 all-reduce.6
  225.5 50.6 all-reduce.8
  281.2 71.0 all-reduce.10
  384.2 101.5 all-reduce.12
  507.9 50.6 all-reduce.14
  563.6 71.0 all-reduce.16
